TPU v7x, 32 devices: a whole 2x2x4 slice. The times are simulated.
32 devices in a mesh: seq: 16 (over z, y, x), dp: 2 (over core).
Axes of the slice: x: 2, y: 2, z: 4, core: 2. Of those that a mesh axis runs over, the one named last changes fastest.
Arguments:
- inputs: bfloat16 [8, 1536, 896], P('dp', 'seq'), may hold values from -6 to 6
- lengths: int32 [8, 9], P('dp'), may hold values from 0 to 1536, as said below
- w_qkv: bfloat16 [896, 1152], replicated, may hold values from -0.1875 to 0.1875
- b_qkv: bfloat16 [1152], replicated, may hold values from -3 to 3
- g_attn: bfloat16 [896], replicated, may hold values from 0.25 to 1.75
- w_out: bfloat16 [896, 896], replicated, may hold values from -1.5 to 1.5
- g_mlp: bfloat16 [896], replicated, may hold values from 0.25 to 1.75
- w_gate_up: bfloat16 [896, 9728], replicated, may hold values from -0.1875 to 0.1875
- w_down: bfloat16 [4864, 896], replicated, may hold values from -0.078125 to 0.078125
- cotangent: bfloat16 [8, 1536, 896], P('dp', 'seq'), may hold values from -6 to 6
Outputs:
- output: bfloat16 [8, 1536, 896], P('dp', 'seq')
- grad_input: float32 [8, 1536, 896], P('dp', 'seq')
- grad_qkv: float32 [896, 1152], P('seq')
- grad_bias_qkv: float32 [1152], replicated
- grad_norm_attn: float32 [896], replicated
- grad_out: float32 [896, 896], P('seq')
- grad_norm_mlp: float32 [896], replicated
- grad_gate_up: float32 [896, 9728], P('seq')
- grad_down: float32 [4864, 896], P('seq')
Inputs may be any that keep to these rules, and one draw needn't show every extreme that they name: Each row lists the lengths of the documents packed one after another from the start of a stream; nonzero entries come first, and the tokens after their sum, fewer than 96, are padding. In every group of 4 consecutive rows one row is a single document of 1536 tokens; any other document has at most 4096 tokens.
All inputs are finite; a program needn't handle non-finite values.
Results may differ from a plain program's by a relative error of at most 0.014.
Values may be sent and summed in bfloat16 or wider, within the bound.
No kernel may reach another device: no remote copies, remote signals or barrier semaphores. Data moves between devices by JAX's collectives and lax.ppermute only.
A program may use at most 576 MiB of HBM per device.

v0:
```python
import jax
import jax.numpy as jnp
from jax import lax
from jax.sharding import PartitionSpec as P

HEADS = 14
KVH = 2
HD = 64
FF = 4864
epsilon = 1e-06
rope_base = 1000000.0


def cut_along(shard, dim, devices):
    before, after = (shard.shape[:dim], shard.shape[dim + 1 :])
    return jnp.moveaxis(shard.reshape(*before, devices, -1, *after), dim, 0)


def summed_on_arrival(shard, axis, dim):
    devices = lax.axis_size(axis)
    blocks = lax.all_to_all(cut_along(shard, dim, devices), axis, 0, 0, tiled=True)
    return jnp.sum(blocks.astype(jnp.float32), axis=0)


def layout(lengths, offset, row_count):
    places = offset + jnp.arange(row_count, dtype=jnp.int32)
    ends = jnp.cumsum(lengths, axis=-1, dtype=jnp.int32)
    after = (places[None, :, None] >= ends[:, None, :]).astype(jnp.int32)
    segment = jnp.sum(after, axis=-1, dtype=jnp.int32)
    begins = jnp.sum(after * lengths[:, None, :], axis=-1, dtype=jnp.int32)
    return (segment, places[None, :] - begins, places[None, :] < ends[:, -1:])


def tables(position, head_size):
    half = head_size // 2
    inverse = rope_base ** (-(jnp.arange(half, dtype=jnp.float32) * (2.0 / head_size)))
    angle = position.astype(jnp.float32)[..., None] * inverse
    return (jnp.cos(angle)[..., None, :], jnp.sin(angle)[..., None, :])


def rotate(field, cos_table, sin_table):
    half = field.shape[-1] // 2
    first = field[..., :half]
    second = field[..., half:]
    return jnp.concatenate(
        [first * cos_table - second * sin_table, second * cos_table + first * sin_table], axis=-1
    )


def unrotate(grad_field, cos_table, sin_table):
    half = grad_field.shape[-1] // 2
    first = grad_field[..., :half]
    second = grad_field[..., half:]
    return jnp.concatenate(
        [first * cos_table + second * sin_table, second * cos_table - first * sin_table], axis=-1
    )


def transposed_product(left, right):
    return lax.dot_general(
        left, right, (((1,), (1,)), ((), ())), preferred_element_type=jnp.float32
    )


def shards(inputs, lengths, w_qkv, b_qkv, g_attn, w_out, g_mlp, w_gate_up, w_down, cotangent):
    streams, length, model_width = inputs.shape
    tokens = streams * length
    stream_len = length * lax.axis_size("seq")
    offset = lax.axis_index("seq") * length
    q_width = HEADS * HD
    kv_width = KVH * HD
    group_size = HEADS // KVH
    factor = HD ** (-0.5)
    blocks = max(1, min(16, stream_len // 512))
    key_block = stream_len // blocks
    q_seg, q_pos, valid_rows = layout(lengths, offset, length)
    k_seg, unused_pos, unused_valid = layout(lengths, 0, stream_len)
    q_place = offset + jnp.arange(length, dtype=jnp.int32)
    residual = inputs.reshape(tokens, model_width).astype(jnp.float32)
    inv_attn = lax.rsqrt(jnp.mean(residual * residual, axis=-1, keepdims=True) + epsilon)
    unit_attn = residual * inv_attn
    gain_attn = g_attn.astype(jnp.float32)
    normed = (unit_attn * gain_attn).astype(jnp.bfloat16)
    projected = jnp.dot(normed, w_qkv, preferred_element_type=jnp.float32) + b_qkv.astype(
        jnp.float32
    )
    cos_table, sin_table = tables(q_pos.reshape(tokens), HD)
    q_rot = rotate(projected[:, :q_width].reshape(tokens, HEADS, HD), cos_table, sin_table)
    k_rot = rotate(
        projected[:, q_width : q_width + kv_width].reshape(tokens, KVH, HD), cos_table, sin_table
    )
    queries = q_rot.astype(jnp.bfloat16).reshape(streams, length, KVH, group_size, HD)
    key_low = k_rot.astype(jnp.bfloat16).reshape(streams, length, kv_width)
    value_low = (
        projected[:, q_width + kv_width :].astype(jnp.bfloat16).reshape(streams, length, kv_width)
    )
    key_all, value_all = (
        lax.all_gather(key_low, "seq", axis=1, tiled=True),
        lax.all_gather(value_low, "seq", axis=1, tiled=True),
    )
    key_all = key_all.reshape(streams, stream_len, KVH, HD)
    value_all = value_all.reshape(streams, stream_len, KVH, HD)

    def scored(key_part, key_seg, first_key, rows):
        scores = (
            jnp.einsum("bqhgd,bkhd->bhgqk", queries, key_part, preferred_element_type=jnp.float32)
            * factor
        )
        key_place = first_key + jnp.arange(rows, dtype=jnp.int32)
        allowed = (q_seg[:, :, None] == key_seg[:, None, :]) & (
            q_place[None, :, None] >= key_place[None, None, :]
        )
        return (scores, allowed[:, None, None])

    def touches(first_key, rows):
        last_seg = lax.dynamic_slice_in_dim(k_seg, first_key + rows - 1, 1, 1)[:, 0]
        return jnp.any((first_key <= q_place[length - 1]) & (last_seg >= q_seg[:, 0]))

    def slices(first_key, rows, key_src, value_src):
        return (
            lax.dynamic_slice_in_dim(key_src, first_key, rows, 1),
            lax.dynamic_slice_in_dim(value_src, first_key, rows, 1),
            lax.dynamic_slice_in_dim(k_seg, first_key, rows, 1),
        )

    def softmax_stats(block_index, running):
        first_key = block_index * key_block

        def softmax_compute(state):
            row_max, row_sum = state
            key_part, unused_value, key_seg = slices(first_key, key_block, key_all, value_all)
            scores, allowed = scored(key_part, key_seg, first_key, key_block)
            masked = jnp.where(allowed, scores, -1e30)
            new_max = jnp.maximum(row_max, jnp.max(masked, axis=-1, keepdims=True))
            fresh = jnp.where(allowed, jnp.exp(masked - new_max), 0.0)
            return (
                new_max,
                row_sum * jnp.exp(row_max - new_max) + jnp.sum(fresh, axis=-1, keepdims=True),
            )

        return lax.cond(
            touches(first_key, key_block), softmax_compute, lambda state: state, running
        )

    stat_shape = (streams, KVH, group_size, length, 1)
    row_max, row_sum = lax.fori_loop(
        0,
        blocks,
        softmax_stats,
        (jnp.full(stat_shape, -1e30, jnp.float32), jnp.zeros(stat_shape, jnp.float32)),
    )
    log_sum = row_max + jnp.log(row_sum)

    def weighted(block_index, running):
        first_key = block_index * key_block

        def weighted_compute(partial_value):
            key_part, value_part, key_seg = slices(first_key, key_block, key_all, value_all)
            scores, allowed = scored(key_part, key_seg, first_key, key_block)
            weights = jnp.where(allowed, jnp.exp(scores - log_sum), 0.0).astype(jnp.bfloat16)
            return partial_value + jnp.einsum(
                "bhgqk,bkhd->bqhgd", weights, value_part, preferred_element_type=jnp.float32
            )

        return lax.cond(
            touches(first_key, key_block),
            weighted_compute,
            lambda partial_value: partial_value,
            running,
        )

    mixed_out = lax.fori_loop(
        0, blocks, weighted, jnp.zeros((streams, length, KVH, group_size, HD), jnp.float32)
    )
    mixed_low = mixed_out.reshape(tokens, q_width).astype(jnp.bfloat16)
    middle = residual + jnp.dot(mixed_low, w_out, preferred_element_type=jnp.float32)
    inv_mlp = lax.rsqrt(jnp.mean(middle * middle, axis=-1, keepdims=True) + epsilon)
    unit_mlp = middle * inv_mlp
    gain_mlp = g_mlp.astype(jnp.float32)
    normed_mlp = (unit_mlp * gain_mlp).astype(jnp.bfloat16)
    gate_up = jnp.dot(normed_mlp, w_gate_up, preferred_element_type=jnp.float32)
    gate_pre = gate_up[:, :FF]
    up_pre = gate_up[:, FF:]
    gate_sigmoid = jax.nn.sigmoid(gate_pre)
    gate_silu = jax.nn.silu(gate_pre)
    active = (gate_silu * up_pre).astype(jnp.bfloat16)
    output = (middle + jnp.dot(active, w_down, preferred_element_type=jnp.float32)).astype(
        jnp.bfloat16
    )
    seed_grad = (cotangent * valid_rows[..., None].astype(jnp.bfloat16)).reshape(
        tokens, model_width
    )
    grad_active = transposed_product(seed_grad, w_down)
    grad_gate = grad_active * up_pre * (gate_sigmoid * (1.0 + gate_pre * (1.0 - gate_sigmoid)))
    grad_up = grad_active * gate_silu
    grad_gate_up = jnp.concatenate([grad_gate, grad_up], axis=1).astype(jnp.bfloat16)
    grad_normed_mlp = transposed_product(grad_gate_up, w_gate_up)
    scaled_mlp = grad_normed_mlp * gain_mlp
    grad_middle = seed_grad.astype(jnp.float32) + inv_mlp * (
        scaled_mlp - unit_mlp * jnp.mean(scaled_mlp * unit_mlp, axis=-1, keepdims=True)
    )
    gain_mlp_part = jnp.sum(grad_normed_mlp * unit_mlp, axis=0)
    grad_branch = grad_middle.astype(jnp.bfloat16)
    grad_mixed = (
        transposed_product(grad_branch, w_out)
        .astype(jnp.bfloat16)
        .reshape(streams, length, KVH, group_size, HD)
    )
    row_delta = jnp.sum(grad_mixed.astype(jnp.float32) * mixed_out, axis=-1).transpose(0, 2, 3, 1)[
        ..., None
    ]
    key_back, value_back = (
        lax.all_gather(key_low, "seq", axis=1, tiled=True),
        lax.all_gather(value_low, "seq", axis=1, tiled=True),
    )
    key_back = key_back.reshape(streams, stream_len, KVH, HD)
    value_back = value_back.reshape(streams, stream_len, KVH, HD)

    def back_block(block_index, running):
        first_key = block_index * key_block

        def back_compute(state):
            query_grads, key_terms_all = state
            key_part, value_part, key_seg = slices(first_key, key_block, key_back, value_back)
            scores, allowed = scored(key_part, key_seg, first_key, key_block)
            weights = jnp.where(allowed, jnp.exp(scores - log_sum), 0.0)
            grad_weights = jnp.einsum(
                "bqhgd,bkhd->bhgqk", grad_mixed, value_part, preferred_element_type=jnp.float32
            )
            grad_scores = (weights * (grad_weights - row_delta)).astype(jnp.bfloat16)
            query_grads = (
                query_grads
                + jnp.einsum(
                    "bhgqk,bkhd->bqhgd", grad_scores, key_part, preferred_element_type=jnp.float32
                )
                * factor
            )
            grad_keys = (
                jnp.einsum(
                    "bhgqk,bqhgd->kbhd", grad_scores, queries, preferred_element_type=jnp.float32
                )
                * factor
            )
            grad_values = jnp.einsum(
                "bhgqk,bqhgd->kbhd",
                weights.astype(jnp.bfloat16),
                grad_mixed,
                preferred_element_type=jnp.float32,
            )
            piece = jnp.concatenate(
                [
                    grad_keys.reshape(key_block, streams, kv_width),
                    grad_values.reshape(key_block, streams, kv_width),
                ],
                axis=-1,
            )
            key_terms_all = lax.dynamic_update_slice_in_dim(key_terms_all, piece, first_key, 0)
            return (query_grads, key_terms_all)

        return lax.cond(touches(first_key, key_block), back_compute, lambda state: state, running)

    grad_queries, key_terms_all = lax.fori_loop(
        0,
        blocks,
        back_block,
        (
            jnp.zeros((streams, length, KVH, group_size, HD), jnp.float32),
            jnp.zeros((stream_len, streams, 2 * kv_width), jnp.float32),
        ),
    )
    key_grads = summed_on_arrival(key_terms_all.astype(jnp.bfloat16), "seq", 0)
    key_grads = key_grads.transpose(1, 0, 2).reshape(tokens, 2 * kv_width)
    grad_q_lin = unrotate(grad_queries.reshape(tokens, HEADS, HD), cos_table, sin_table).reshape(
        tokens, q_width
    )
    grad_k_lin = unrotate(
        key_grads[:, :kv_width].reshape(tokens, KVH, HD), cos_table, sin_table
    ).reshape(tokens, kv_width)
    grad_projected = jnp.concatenate(
        [grad_q_lin, grad_k_lin, key_grads[:, kv_width:]], axis=1
    ).astype(jnp.bfloat16)
    grad_normed = transposed_product(grad_projected, w_qkv)
    scaled_attn = grad_normed * gain_attn
    grad_input = grad_middle + inv_attn * (
        scaled_attn - unit_attn * jnp.mean(scaled_attn * unit_attn, axis=-1, keepdims=True)
    )
    gain_attn_part = jnp.sum(grad_normed * unit_attn, axis=0)
    bias_part = jnp.sum(grad_projected.astype(jnp.float32), axis=0)

    def make_rows():

        def product(left, right):
            return lax.dot_general(
                left, right, (((0,), (0,)), ((), ())), preferred_element_type=jnp.float32
            )

        def row_terms(first_col, col_count):
            return jnp.concatenate(
                [
                    product(normed, grad_projected),
                    product(mixed_low, grad_branch),
                    product(normed_mlp, grad_gate_up),
                ],
                axis=1,
            )

        def down_terms(first_col, col_count):
            return product(active, seed_grad)

        return (row_terms, down_terms)

    row_share = model_width // lax.axis_size("seq")
    hidden_share = FF // lax.axis_size("seq")
    row_terms, down_terms = make_rows()
    row_part = lax.psum_scatter(
        row_terms(jnp.int32(0), row_share * lax.axis_size("seq")),
        "seq",
        scatter_dimension=0,
        tiled=True,
    )
    down_part = summed_on_arrival(
        down_terms(jnp.int32(0), hidden_share * lax.axis_size("seq")).astype(jnp.bfloat16), "seq", 0
    )
    row_part, down_part = (
        lax.psum(row_part.astype(jnp.bfloat16), "dp").astype(jnp.float32),
        lax.psum(down_part.astype(jnp.bfloat16), "dp").astype(jnp.float32),
    )
    bias_grad, gain_attn_grad, gain_mlp_grad = lax.psum(
        (bias_part, gain_attn_part, gain_mlp_part), ("seq", "dp")
    )
    joined_width = q_width + 2 * kv_width
    return (
        output.reshape(streams, length, model_width),
        grad_input.reshape(streams, length, model_width),
        row_part[:, :joined_width],
        bias_grad,
        gain_attn_grad,
        row_part[:, joined_width : joined_width + model_width],
        gain_mlp_grad,
        row_part[:, joined_width + model_width :],
        down_part,
    )


def solution(mesh):
    in_specs = (
        P("dp", "seq", None),
        P("dp", None),
        P(),
        P(),
        P(),
        P(),
        P(),
        P(),
        P(),
        P("dp", "seq", None),
    )
    out_specs = (
        P("dp", "seq", None),
        P("dp", "seq", None),
        P("seq", None),
        P(),
        P(),
        P("seq", None),
        P(),
        P("seq", None),
        P("seq", None),
    )
    return jax.shard_map(shards, mesh=mesh, in_specs=in_specs, out_specs=out_specs, check_vma=False)
```

profile of v0, /device:TPU:6, one launch (start us, length us, event | category | flops | bytes accessed | tf_op | source)
XLA Modules:
  0.0 1464.1 jit_solution(16891637317464104812)
XLA Ops:
  29.2 46.4 %all-gather.5.cloned.1.call-done = bf16[4,1536,128]{2,0,1:T(4,128)(2,1)} async-done(((bf16[4,96,128]{2,0,1:T(4,128)(2,1)}), bf16[4,1536,128]{2,0,1:T(4,128)(2,1)}) %all-gather.5.cloned.1.call-update) | async-done | bytes 1572880 | tf_op jit(solution)/shard_map/all_gather | solution.py:98
  75.6 3.9 copy.106
  79.5 15.1 %while.58 = (s32[]{:T(128)}, f32[4,2,7,96,1]{3,2,1,0,4:T(8,128)S(1)}, f32[4,2,7,96,1]{3,2,1,0,4:T(8,128)S(1)}, s32[96]{0:T(128)S(1)}, s32[4,1536]{1,0:T(4,128)S(...) while((s32[]{:T(128)}, ...), condition=%wide.region_11.12_spmd, body=%wide.region_5.11_spmd.sunk | while | flops 374795296 | bytes 24231176 | solution.py:146
  82.1 7.2 conditional.6
  82.5 3.3 fusion
  85.8 3.5 select_reduce_fusion
  94.6 40.9 %all-gather.3.cloned.1.call-done = bf16[4,1536,128]{2,1,0:T(8,128)(2,1)} async-done(((bf16[4,96,128]{2,1,0:T(8,128)(2,1)}), bf16[4,1536,128]{2,1,0:T(8,128)(2,1)}) %all-gather.3.cloned.1.call-update) | async-done | bytes 1572880 | tf_op jit(solution)/shard_map/all_gather | solution.py:99
  139.5 15.9 %while.59 = (s32[]{:T(128)}, f32[4,96,2,7,64]{1,4,3,2,0:T(8,128)}, s32[96]{0:T(128)S(1)}, s32[4,1536]{1,0:T(4,128)S(1)}, s32[4,96]{1,0:T(4,128)S(1)}, /*index=5*...) while((s32[]{:T(128)}, f32[4,96,2,7,64]{1,4,3,2,0:T(8,128)}, ...), condition=%wide.region_16.17_spmd, body=%wide.region_12.16_spmd.sunk | while | flops 716440064 | bytes 5492981 | solution.py:172
  142.1 8.1 conditional.7
  142.5 7.7 bitcast_add_fusion.1
  164.3 17.4 %fusion.57 = f32[384,9728]{1,0:T(8,128)} fusion(bf16[896,9728]{1,0:T(8,128)(2,1)} %param.29, f32[384,896]{1,0:T(8,128)S(1)} %get-tuple-element.1328, f32[896]{0:T(1024)S(1)} %convert_element_type.166, f32[384]{0:T(512)S(1)} %add_rsqrt_fusion), kind=kOutput, calls=%fused_computation.134 | convolution fusion | flops 6695141376 | bytes 33756160 | tf_op jit(solution)/shard_map/dot_general | solution.py:181
  181.7 14.5 multiply_convert_fusion.1
  196.2 16.0 %multiply_reduce_fusion = (f32[896]{0:T(1024)}, f32[384]{0:T(512)S(1)}, f32[384,896]{1,0:T(8,128)}) fusion(f32[384,896]{1,0:T(8,128)} %copy-done.8, f32[384]{0:T(512)S(1)} %add_rsqrt_fusion, f32[896]{0:T(1024)S(1)} %convert_element_type.166, bf16[896,9728]{1,0:T(8,128)(2,1)} %param.29, bf16[384,4864]{1,0:T(8,128)(2,1)} %get-tuple-element.1315, ...), kind=kOutput, calls=%fused_computation.84 | convolution fusion | flops 6711114240 | bytes 27666432 | tf_op jit(solution)/shard_map/dot_general | solution.py:60
  219.9 3.4 reshape.367
  223.3 3.3 fusion.49
  231.2 25.8 %while.60 = (s32[]{:T(128)}, f32[4,96,2,7,64]{1,4,3,2,0:T(8,128)}, bf16[1536,4,256]{0,2,1:T(8,128)(2,1)}, s32[96]{0:T(128)S(1)}, s32[4,1536]{1,0:T(4,128)S(1)}, ...) while((s32[]{:T(128)}, f32[4,96,2,7,64]{1,4,3,2,0:T(8,128)}, ...), condition=%wide.region_24.25_spmd, body=%wide.region_20.24_spmd.sunk | while | flops 1792885248 | bytes 74315176 | solution.py:262
  233.8 18.0 %conditional.8 = ((f32[4,96,2,7,64]{1,4,3,2,0:T(8,128)}, bf16[1536,4,256]{0,2,1:T(8,128)(2,1)})) conditional(s32[]{:T(128)} %convert_element_type.222, (f32[4,96,2,7,64]{1,4,3,2,0:T(8,128)}, bf16[1536,4,256]{0,2,1:T(8,128)(2,1)}) %tuple.195, (s32[]{:T(128)}, bf16[4,1536,2,64]{1,3,2,0:T(8,128)(2,1)}, s32[4,96]{1,0:T(4,128)S(1)}, ...), branch_computations={%region_22.22_spmd, %region_23.23_spmd} | conditional | flops 1792885248 | bytes 74314792 | solution.py:260
  239.8 5.0 fusion.26
  257.0 4.7 copy.117
  261.7 3.8 copy.118
  265.6 57.8 %all-to-all-start = ((bf16[16,96,4,256]{3,1,2,0:T(8,128)(2,1)}), bf16[16,96,4,256]{3,1,2,0:T(8,128)(2,1)}, u32[]{:S(2)}, u32[]{:S(2)}) async-start(bf16[16,96,4,256]{3,1,2,0:T(8,128)(2,1)} %copy.118), calls=%async_computation | async-start | bytes 6291456 | tf_op jit(solution)/shard_map/all_to_all | solution.py:21
  323.4 3.9 copy.116
  335.8 18.5 %fusion.47 = f32[896,9728]{1,0:T(8,128)} fusion(bf16[384,4864]{1,0:T(8,128)(2,1)} %get-tuple-element.1315, bf16[384,4864]{1,0:T(8,128)(2,1)} %get-tuple-element.1314, f32[384,896]{1,0:T(8,128)} %copy-done.8, f32[896]{0:T(1024)S(1)} %convert_element_type.166, f32[384]{0:T(512)S(1)} %add_rsqrt_fusion), kind=kOutput, calls=%fused_computation.76 | convolution fusion | flops 6710083584 | bytes 43717632 | tf_op jit(solution)/shard_map/dot_general | solution.py:293
  354.3 31.3 %all-to-all-done = bf16[16,96,4,256]{3,1,2,0:T(8,128)(2,1)} async-done(((bf16[16,96,4,256]{3,1,2,0:T(8,128)(2,1)}), bf16[16,96,4,256]{3,1,2,0:T(8,128)(2,1)}, u32[]{:S(2)}, u32[]{:S(2)}) %all-to-all-start) | async-done | bytes 3145760 | tf_op jit(solution)/shard_map/all_to_all | solution.py:21
  393.8 4.8 fusion.58
  398.6 29.1 %pad_maximum_fusion = f32[896,11776]{1,0:T(8,128)} fusion(f32[896,9728]{1,0:T(8,128)} %fusion.47, f32[896,896]{1,0:T(8,128)} %fusion.50, f32[896,1152]{1,0:T(8,128)} %fusion.58), kind=kLoop, calls=%fused_computation.67 | loop fusion | flops 21102592 | bytes 84410368 | tf_op jit(solution)/shard_map/concatenate | solution.py:298
  427.8 7.2 convolution_convert_fusion
  435.0 292.5 %all_to_all.10 = bf16[16,304,896]{2,1,0:T(8,128)(2,1)} all-to-all(bf16[16,304,896]{2,1,0:T(8,128)(2,1)S(1)} %bitcast.171), channel_id=1, replica_groups=mesh['seq'=16,'dp'=2] {'seq'}, dimensions={0} | all-to-all | bytes 17432576 | tf_op jit(solution)/shard_map/all_to_all | solution.py:21
  727.4 5.8 reduce_sum.141
  733.2 653.0 %reduce-scatter.2.cloned.1.call-done = f32[56,11776]{1,0:T(8,128)} async-done(((f32[896,11776]{1,0:T(8,128)}), f32[56,11776]{1,0:T(8,128)}) %reduce-scatter.2.cloned.1.call-update) | async-done | bytes 2637840 | tf_op jit(solution)/shard_map/reduce_scatter | solution.py:315
  1389.3 9.9 add_convert_fusion
  1402.4 44.2 %all-reduce = (f32[1152]{0:T(1024)}, f32[896]{0:T(1024)}, f32[896]{0:T(1024)}) all-reduce(f32[1152]{0:T(1024)S(1)} %convert_reduce_fusion.1, f32[896]{0:T(1024)} %get-tuple-element.1245, f32[896]{0:T(1024)} %get-tuple-element.1243), channel_id=1, replica_groups=mesh['seq'=16,'dp'=2] {'seq','dp'}, use_global_device_ids=true, to_apply=%region_30.31 | all-reduce | flops 2944 | bytes 23552 | tf_op jit(solution)/shard_map/psum | solution.py:328
  (184 shorter events, 105.6 us)
Async XLA Ops:
  7.2 6.3 copy-start
  7.2 68.4 %all-gather.5.cloned.1.call-start = ((), (), s32[]{:S(2)}) async-start(), calls=%async_computation.4 | async-start | bytes 1671168 | tf_op jit(solution)/shard_map/all_gather | solution.py:98
  10.4 4.2 copy-start.25
  11.1 3.5 copy-start.23
  11.2 3.4 copy-start.21
  14.7 1.2 copy-start.12
  16.0 5.4 copy-start.27
  16.3 6.9 copy-start.13
  16.3 6.9 copy-start.15
  17.3 118.2 %all-gather.3.cloned.1.call-start = ((), (), s32[]{:S(2)}) async-start(), calls=%async_computation.3 | async-start | bytes 1671168 | tf_op jit(solution)/shard_map/all_gather | solution.py:99
  25.6 2.4 copy-start.22
  26.8 1.4 copy-start.19
  164.2 17.5 %copy-start.8 = (f32[384,896]{1,0:T(8,128)}, f32[384,896]{1,0:T(8,128)S(1)}, u32[]{:S(2)}) copy-start(f32[384,896]{1,0:T(8,128)S(1)} %get-tuple-element.1328) | copy-start | bytes 4128772
  164.3 17.4 %copy-start.10 = (bf16[4,96,896]{2,1,0:T(8,128)(2,1)S(1)}, bf16[4,96,896]{2,1,0:T(8,128)(2,1)}, u32[]{:S(2)}) copy-start(bf16[4,96,896]{2,1,0:T(8,128)(2,1)} %broadcast_multiply_fusion) | copy-start | bytes 2064388
  212.2 3.6 copy-start.28
  223.3 3.4 copy-start.5
  234.2 2.8 copy-start.17
  244.9 1.5 copy-start.1
  249.5 1.2 copy-start.2
  265.6 120.0 %all-to-all-start = ((bf16[16,96,4,256]{3,1,2,0:T(8,128)(2,1)}), bf16[16,96,4,256]{3,1,2,0:T(8,128)(2,1)}, u32[]{:S(2)}, u32[]{:S(2)}) async-start(bf16[16,96,4,256]{3,1,2,0:T(8,128)(2,1)} %copy.118), calls=%async_computation | async-start | bytes 6291456 | tf_op jit(solution)/shard_map/all_to_all | solution.py:21
  323.3 1063.0 %reduce-scatter.2.cloned.1.call-start = ((), (), s32[]{:S(2)}) async-start(), calls=%async_computation.5 | async-start | bytes 44843008 | tf_op jit(solution)/shard_map/reduce_scatter | solution.py:315
  327.3 3.1 copy-start.14
  327.3 3.1 copy-start.16
  330.4 2.6 copy-start.4
  330.4 2.6 copy-start.11
  427.7 1022.6 %all-reduce.4.cloned.1.call-start = ((), (), s32[]{:S(2)}) async-start(), calls=%async_computation.6 | async-start | bytes 3727360 | tf_op jit(solution)/shard_map/psum | solution.py:325
  1389.2 9.9 copy-start.7
  1389.2 9.9 copy-start.18
  1389.3 10.2 copy-start.6
  1389.3 10.2 copy-start.24
  1389.3 10.1 copy-start.26
  1453.5 2.8 copy-start.20
  (2 other events, 2.4 us)
Sparse Core Ops, SparseCore 0:
  17.4 58.1 all-gather.4
  78.8 56.6 all-gather.2
  427.9 958.3 reduce-scatter.1
  1389.4 22.3 all-reduce.3
where the time goes:
time: 1470 us; the launch traced here: 1460 us
  waiting for transfers between devices  772 us (53%)
  blocking collectives  337 us (23%)
  matrix products  126 us (9%)
  other arithmetic  76.5 us (5%)
  local copies, waits for them, and re-layouts  68.9 us (5%)
  starting transfers between devices  57.9 us (4%)
    reduce_scatter x1, waiting for transfers between devices, shards(): lax.psum_scatter(row_terms(jnp.int32(0), row_share * lax.axis_size('seq')...  653 us
    all_to_all x1, blocking collectives, summed_on_arrival(): lax.all_to_all(cut_along(shard, dim, devices), axis, 0, 0, tiled=True)  292 us
    all_to_all x1, starting transfers between devices, summed_on_arrival(): lax.all_to_all(cut_along(shard, dim, devices), axis, 0, 0, tiled=True)  57.8 us
    all_gather x1, waiting for transfers between devices, shards(): lax.all_gather(key_low, 'seq', axis=1, tiled=True)  46.4 us
    psum x1, blocking collectives, shards(): lax.psum((bias_part, gain_attn_part, gain_mlp_part), ('seq', 'dp'))  44.2 us
    all_gather x1, waiting for transfers between devices, shards(): lax.all_gather(value_low, 'seq', axis=1, tiled=True)  40.9 us
    dot_general x4, matrix products, transposed_product(): lax.dot_general(left, right, (((1,), (1,)), ((), ())), preferred_element_...  35.4 us
    dot_general x4, matrix products, product(): lax.dot_general(left, right, (((0,), (0,)), ((), ())), preferred_element_...  33.2 us
  transfers between devices with their start and end apart: 5, of which 4 were waited for; matrix products, arithmetic and copies ran while one was open for 6% of the time, Pallas kernels for 0%

commit v1 on v0

--- a/solution.py
+++ b/solution.py
@@ -326,7 +326,7 @@
         lax.psum(down_part.astype(jnp.bfloat16), "dp").astype(jnp.float32),
     )
     bias_grad, gain_attn_grad, gain_mlp_grad = lax.psum(
-        (bias_part, gain_attn_part, gain_mlp_part), ("seq", "dp")
+        lax.psum((bias_part, gain_attn_part, gain_mlp_part), "dp"), "seq"
     )
     joined_width = q_width + 2 * kv_width
     return (

time: 1470 us -> 1500 us (1.020)
  blocking collectives: 337 us -> 363 us
    psum x1 -> x2, blocking collectives: 44.2 us -> 71.8 us  [the longest x1 68.5 us: shards(): lax.psum(lax.psum((bias_part, gain_attn_part, gain_mlp_part), 'dp'), 'seq')]
where the time goes in v1:
time: 1500 us; the launch traced here: 1490 us
  waiting for transfers between devices  772 us (51%)
  blocking collectives  363 us (24%)
  matrix products  126 us (8%)
  other arithmetic  74.7 us (5%)
  local copies, waits for them, and re-layouts  64.7 us (4%)
  starting transfers between devices  57.9 us (4%)
    reduce_scatter x1, waiting for transfers between devices, shards(): lax.psum_scatter(row_terms(jnp.int32(0), row_share * lax.axis_size('seq')...  653 us
    all_to_all x1, blocking collectives, summed_on_arrival(): lax.all_to_all(cut_along(shard, dim, devices), axis, 0, 0, tiled=True)  291 us
    psum x1, blocking collectives, shards(): lax.psum(lax.psum((bias_part, gain_attn_part, gain_mlp_part), 'dp'), 'seq')  68.5 us
    all_to_all x1, starting transfers between devices, summed_on_arrival(): lax.all_to_all(cut_along(shard, dim, devices), axis, 0, 0, tiled=True)  57.8 us
    all_gather x1, waiting for transfers between devices, shards(): lax.all_gather(key_low, 'seq', axis=1, tiled=True)  46.8 us
    all_gather x1, waiting for transfers between devices, shards(): lax.all_gather(value_low, 'seq', axis=1, tiled=True)  40.9 us
    dot_general x4, matrix products, transposed_product(): lax.dot_general(left, right, (((1,), (1,)), ((), ())), preferred_element_...  34.8 us
    dot_general x4, matrix products, product(): lax.dot_general(left, right, (((0,), (0,)), ((), ())), preferred_element_...  33.7 us
  transfers between devices with their start and end apart: 5, of which 4 were waited for; matrix products, arithmetic and copies ran while one was open for 6% of the time, Pallas kernels for 0%

profile of v1, /device:TPU:6, one launch (start us, length us, event | category | flops | bytes accessed | tf_op | source)
XLA Modules:
  0.0 1485.1 jit_solution(12301720233843938556)
XLA Ops:
  28.8 46.8 %all-gather.5.cloned.1.call-done = bf16[4,1536,128]{2,0,1:T(4,128)(2,1)} async-done(((bf16[4,96,128]{2,0,1:T(4,128)(2,1)}), bf16[4,1536,128]{2,0,1:T(4,128)(2,1)}) %all-gather.5.cloned.1.call-update) | async-done | bytes 1572880 | tf_op jit(solution)/shard_map/all_gather | solution.py:98
  75.5 3.9 copy.106
  79.5 15.1 %while.58 = (s32[]{:T(128)}, f32[4,2,7,96,1]{3,2,1,0,4:T(8,128)S(1)}, f32[4,2,7,96,1]{3,2,1,0,4:T(8,128)S(1)}, s32[96]{0:T(128)S(1)}, s32[4,1536]{1,0:T(4,128)S(...) while((s32[]{:T(128)}, ...), condition=%wide.region_11.12_spmd, body=%wide.region_5.11_spmd.sunk | while | flops 374795296 | bytes 24231176 | solution.py:146
  82.1 7.1 conditional.6
  85.7 3.5 select_reduce_fusion
  94.6 40.9 %all-gather.3.cloned.1.call-done = bf16[4,1536,128]{2,1,0:T(8,128)(2,1)} async-done(((bf16[4,96,128]{2,1,0:T(8,128)(2,1)}), bf16[4,1536,128]{2,1,0:T(8,128)(2,1)}) %all-gather.3.cloned.1.call-update) | async-done | bytes 1572880 | tf_op jit(solution)/shard_map/all_gather | solution.py:99
  139.5 15.9 %while.59 = (s32[]{:T(128)}, f32[4,96,2,7,64]{1,4,3,2,0:T(8,128)}, s32[96]{0:T(128)S(1)}, s32[4,1536]{1,0:T(4,128)S(1)}, s32[4,96]{1,0:T(4,128)S(1)}, /*index=5*...) while((s32[]{:T(128)}, f32[4,96,2,7,64]{1,4,3,2,0:T(8,128)}, ...), condition=%wide.region_16.17_spmd, body=%wide.region_12.16_spmd.sunk | while | flops 716440064 | bytes 5492981 | solution.py:172
  142.1 8.1 conditional.7
  142.4 7.7 bitcast_add_fusion.1
  164.2 17.4 %fusion.57 = f32[384,9728]{1,0:T(8,128)} fusion(bf16[896,9728]{1,0:T(8,128)(2,1)} %param.29, f32[384,896]{1,0:T(8,128)S(1)} %get-tuple-element.1331, f32[896]{0:T(1024)S(1)} %convert_element_type.166, f32[384]{0:T(512)S(1)} %add_rsqrt_fusion), kind=kOutput, calls=%fused_computation.134 | convolution fusion | flops 6695141376 | bytes 33756160 | tf_op jit(solution)/shard_map/dot_general | solution.py:181
  181.7 14.5 multiply_convert_fusion.1
  196.2 16.0 %multiply_reduce_fusion = (f32[896]{0:T(1024)}, f32[384]{0:T(512)S(1)}, f32[384,896]{1,0:T(8,128)}) fusion(f32[384,896]{1,0:T(8,128)} %copy-done.9, f32[384]{0:T(512)S(1)} %add_rsqrt_fusion, f32[896]{0:T(1024)S(1)} %convert_element_type.166, bf16[896,9728]{1,0:T(8,128)(2,1)} %param.29, bf16[384,4864]{1,0:T(8,128)(2,1)} %get-tuple-element.1318, ...), kind=kOutput, calls=%fused_computation.84 | convolution fusion | flops 6711114240 | bytes 27666432 | tf_op jit(solution)/shard_map/dot_general | solution.py:60
  219.8 3.4 reshape.367
  223.2 3.3 fusion.49
  231.1 25.8 %while.60 = (s32[]{:T(128)}, f32[4,96,2,7,64]{1,4,3,2,0:T(8,128)}, bf16[1536,4,256]{0,2,1:T(8,128)(2,1)}, s32[96]{0:T(128)S(1)}, s32[4,1536]{1,0:T(4,128)S(1)}, ...) while((s32[]{:T(128)}, f32[4,96,2,7,64]{1,4,3,2,0:T(8,128)}, ...), condition=%wide.region_24.25_spmd, body=%wide.region_20.24_spmd.sunk | while | flops 1792885248 | bytes 74315176 | solution.py:262
  233.7 18.0 %conditional.8 = ((f32[4,96,2,7,64]{1,4,3,2,0:T(8,128)}, bf16[1536,4,256]{0,2,1:T(8,128)(2,1)})) conditional(s32[]{:T(128)} %convert_element_type.222, (f32[4,96,2,7,64]{1,4,3,2,0:T(8,128)}, bf16[1536,4,256]{0,2,1:T(8,128)(2,1)}) %tuple.195, (s32[]{:T(128)}, bf16[4,1536,2,64]{1,3,2,0:T(8,128)(2,1)}, s32[4,96]{1,0:T(4,128)S(1)}, ...), branch_computations={%region_22.22_spmd, %region_23.23_spmd} | conditional | flops 1792885248 | bytes 74314792 | solution.py:260
  239.7 5.0 fusion.26
  256.9 4.7 copy.117
  261.6 3.8 copy.118
  265.5 57.8 %all-to-all-start = ((bf16[16,96,4,256]{3,1,2,0:T(8,128)(2,1)}), bf16[16,96,4,256]{3,1,2,0:T(8,128)(2,1)}, u32[]{:S(2)}, u32[]{:S(2)}) async-start(bf16[16,96,4,256]{3,1,2,0:T(8,128)(2,1)} %copy.118), calls=%async_computation | async-start | bytes 6291456 | tf_op jit(solution)/shard_map/all_to_all | solution.py:21
  323.3 3.9 copy.116
  335.0 18.5 %fusion.47 = f32[896,9728]{1,0:T(8,128)} fusion(bf16[384,4864]{1,0:T(8,128)(2,1)} %get-tuple-element.1318, bf16[384,4864]{1,0:T(8,128)(2,1)} %get-tuple-element.1317, f32[384,896]{1,0:T(8,128)} %copy-done.9, f32[896]{0:T(1024)S(1)} %convert_element_type.166, f32[384]{0:T(512)S(1)} %add_rsqrt_fusion), kind=kOutput, calls=%fused_computation.76 | convolution fusion | flops 6710083584 | bytes 43717632 | tf_op jit(solution)/shard_map/dot_general | solution.py:293
  353.5 31.9 %all-to-all-done = bf16[16,96,4,256]{3,1,2,0:T(8,128)(2,1)} async-done(((bf16[16,96,4,256]{3,1,2,0:T(8,128)(2,1)}), bf16[16,96,4,256]{3,1,2,0:T(8,128)(2,1)}, u32[]{:S(2)}, u32[]{:S(2)}) %all-to-all-start) | async-done | bytes 3145760 | tf_op jit(solution)/shard_map/all_to_all | solution.py:21
  388.3 4.6 fusion.58
  393.0 29.1 %pad_maximum_fusion = f32[896,11776]{1,0:T(8,128)} fusion(f32[896,9728]{1,0:T(8,128)} %fusion.47, f32[896,896]{1,0:T(8,128)} %fusion.50, f32[896,1152]{1,0:T(8,128)} %fusion.58), kind=kLoop, calls=%fused_computation.67 | loop fusion | flops 21102592 | bytes 84410368 | tf_op jit(solution)/shard_map/concatenate | solution.py:298
  423.1 7.9 convolution_convert_fusion
  431.0 291.0 %all_to_all.10 = bf16[16,304,896]{2,1,0:T(8,128)(2,1)} all-to-all(bf16[16,304,896]{2,1,0:T(8,128)(2,1)S(1)} %bitcast.171), channel_id=1, replica_groups=mesh['seq'=16,'dp'=2] {'seq'}, dimensions={0} | all-to-all | bytes 17432576 | tf_op jit(solution)/shard_map/all_to_all | solution.py:21
  722.0 5.8 reduce_sum.141
  727.8 652.8 %reduce-scatter.2.cloned.1.call-done = f32[56,11776]{1,0:T(8,128)} async-done(((f32[896,11776]{1,0:T(8,128)}), f32[56,11776]{1,0:T(8,128)}) %reduce-scatter.2.cloned.1.call-update) | async-done | bytes 2637840 | tf_op jit(solution)/shard_map/reduce_scatter | solution.py:315
  1383.6 9.9 add_convert_fusion
  1396.2 3.3 all-reduce.1
  1399.5 68.5 %all-reduce = (f32[1152]{0:T(1024)}, f32[896]{0:T(1024)}, f32[896]{0:T(1024)}) all-reduce(f32[1152]{0:T(1024)S(1)} %get-tuple-element.1310, f32[896]{0:T(1024)S(1)} %get-tuple-element.1311, f32[896]{0:T(1024)S(1)} %get-tuple-element.1312), channel_id=1, replica_groups=mesh['seq'=16,'dp'=2] {'seq'}, use_global_device_ids=true, to_apply=%region_31.32 | all-reduce | flops 2944 | bytes 23552 | tf_op jit(solution)/shard_map/psum | solution.py:328
  (185 shorter events, 102.4 us)
Async XLA Ops:
  7.2 6.3 copy-start
  7.2 68.4 %all-gather.5.cloned.1.call-start = ((), (), s32[]{:S(2)}) async-start(), calls=%async_computation.4 | async-start | bytes 1671168 | tf_op jit(solution)/shard_map/all_gather | solution.py:98
  10.4 4.2 copy-start.24
  11.1 3.5 copy-start.22
  13.5 1.2 copy-start.10
  14.7 1.2 copy-start.14
  16.0 5.4 copy-start.27
  16.3 8.0 copy-start.15
  16.3 8.0 copy-start.17
  17.3 118.2 %all-gather.3.cloned.1.call-start = ((), (), s32[]{:S(2)}) async-start(), calls=%async_computation.3 | async-start | bytes 1671168 | tf_op jit(solution)/shard_map/all_gather | solution.py:99
  26.4 1.4 copy-start.20
  164.2 17.5 %copy-start.9 = (f32[384,896]{1,0:T(8,128)}, f32[384,896]{1,0:T(8,128)S(1)}, u32[]{:S(2)}) copy-start(f32[384,896]{1,0:T(8,128)S(1)} %get-tuple-element.1331) | copy-start | bytes 4128772
  164.2 17.4 %copy-start.11 = (bf16[4,96,896]{2,1,0:T(8,128)(2,1)S(1)}, bf16[4,96,896]{2,1,0:T(8,128)(2,1)}, u32[]{:S(2)}) copy-start(bf16[4,96,896]{2,1,0:T(8,128)(2,1)} %broadcast_multiply_fusion) | copy-start | bytes 2064388
  212.2 3.5 copy-start.28
  223.2 3.4 copy-start.5
  234.1 2.8 copy-start.19
  244.8 1.5 copy-start.1
  249.4 1.2 copy-start.2
  265.5 120.0 %all-to-all-start = ((bf16[16,96,4,256]{3,1,2,0:T(8,128)(2,1)}), bf16[16,96,4,256]{3,1,2,0:T(8,128)(2,1)}, u32[]{:S(2)}, u32[]{:S(2)}) async-start(bf16[16,96,4,256]{3,1,2,0:T(8,128)(2,1)} %copy.118), calls=%async_computation | async-start | bytes 6291456 | tf_op jit(solution)/shard_map/all_to_all | solution.py:21
  323.2 1057.4 %reduce-scatter.2.cloned.1.call-start = ((), (), s32[]{:S(2)}) async-start(), calls=%async_computation.5 | async-start | bytes 44843008 | tf_op jit(solution)/shard_map/reduce_scatter | solution.py:315
  327.2 3.1 copy-start.16
  327.2 3.1 copy-start.18
  330.3 1.8 copy-start.4
  330.3 1.9 copy-start.13
  332.3 56.1 %copy-start.7 = (bf16[384,14,64]{0,2,1:T(8,128)(2,1)}, bf16[384,14,64]{0,2,1:T(8,128)(2,1)S(1)}, u32[]{:S(2)}) copy-start(bf16[384,14,64]{0,2,1:T(8,128)(2,1)S(1)} %pad_maximum_fusion.6) | copy-start | bytes 2064388
  422.1 1049.2 %all-reduce.5.cloned.1.call-start = ((), (), s32[]{:S(2)}) async-start(), calls=%async_computation.6 | async-start | bytes 3727360 | tf_op jit(solution)/shard_map/psum | solution.py:325
  1383.6 9.9 copy-start.8
  1383.6 10.1 copy-start.6
  1383.6 10.1 copy-start.23
  1383.6 10.1 copy-start.25
  1393.8 2.5 copy-start.26
  1474.5 2.8 copy-start.21
  (2 other events, 2.2 us)
Sparse Core Ops, SparseCore 0:
  17.4 58.0 all-gather.4
  78.8 56.6 all-gather.2
  422.2 958.3 reduce-scatter.1
  1383.7 22.2 all-reduce.4
